TPU v7x, 32 devices: a whole 2x2x4 slice. The times are simulated.
32 devices in a mesh: rep: 2 (over core), fsdp: 16 (over z, y, x).
Axes of the slice: x: 2, y: 2, z: 4, core: 2. Of those that a mesh axis runs over, the one named last changes fastest.
Arguments:
- tokens: bfloat16 [16384, 768], P(('rep', 'fsdp')), may hold values from -6 to 6
- valid: int32 [128], P(('rep', 'fsdp')), may hold values from 1 to 192, as said below
- qkv_weight: float32 [2, 768, 2304], P(None, 'fsdp'), may hold values from -0.3125 to 0.3125
- out_weight: float32 [2, 768, 768], P(None, 'fsdp'), may hold values from -0.875 to 0.875
- up_weight: float32 [2, 768, 3072], P(None, 'fsdp'), may hold values from -0.21875 to 0.21875
- down_weight: float32 [2, 3072, 768], P(None, 'fsdp'), may hold values from -0.109375 to 0.109375
- vectors: float32 [2, 9216], P(None, 'fsdp'), may hold values from -0.9 to 1.6, as said below
- cotangent: bfloat16 [16384, 768], P(('rep', 'fsdp')), may hold values from -6 to 6
Outputs:
- layer_out: bfloat16 [16384, 768], P(('rep', 'fsdp'))
- input_grad: float32 [16384, 768], P(('rep', 'fsdp'))
- qkv_grad: float32 [2, 768, 2304], P(None, 'fsdp')
- out_grad: float32 [2, 768, 768], P(None, 'fsdp')
- up_grad: float32 [2, 768, 3072], P(None, 'fsdp')
- down_grad: float32 [2, 3072, 768], P(None, 'fsdp')
- vector_grad: float32 [2, 9216], P(None, 'fsdp')
Inputs may be any that keep to these rules, and one draw needn't show every extreme that they name: `valid`: pair p sits in slot p mod 4 of its group; a pair of a slot of k * 64 rows has more than (k - 1) * 64 real rows; pair 0 fills its slot. `vectors`: norm gains lie between 0.4 and 1.6, the biases between -0.9 and 0.9.
All inputs are finite; a program needn't handle non-finite values.
Results may differ from a plain program's by a relative error of at most 0.029.
The roundings to bfloat16 on the way count: a program that leaves them out, or rounds other values in their place, can miss the bound.
Values may be sent and summed in bfloat16 or wider, within the bound.
No kernel may reach another device: no remote copies, remote signals or barrier semaphores. Data moves between devices by JAX's collectives and lax.ppermute only.
A program may use at most 192 MiB of HBM per device.

v0:
```python
import jax
import jax.numpy as jnp
from jax import lax
from jax.sharding import PartitionSpec as P

HEADS = 12
HD = 64
LAYERS = 2
LEN_UNIT = 64
NORM_EPSILON = 1e-05
NEG_LARGE = -1e30
SCORE_SCALE = 0.125


def slot_layout(valid_groups):
    row_index = jnp.arange(8 * LEN_UNIT, dtype=jnp.int32)
    slot_index = (
        (row_index >= 3 * LEN_UNIT).astype(jnp.int32)
        + (row_index >= 5 * LEN_UNIT).astype(jnp.int32)
        + (row_index >= 7 * LEN_UNIT).astype(jnp.int32)
    )
    slot_start = jnp.where(
        slot_index == 0,
        0,
        jnp.where(
            slot_index == 1, 3 * LEN_UNIT, jnp.where(slot_index == 2, 5 * LEN_UNIT, 7 * LEN_UNIT)
        ),
    ).astype(jnp.int32)
    offset = row_index - slot_start
    slot_pick = (slot_index[:, None] == jnp.arange(4, dtype=jnp.int32)[None, :]).astype(jnp.int32)
    limits = jnp.sum(valid_groups[:, None, :] * slot_pick[None], -1)
    row_live = offset[None, :] < limits
    same_slot = slot_index[:, None] == slot_index[None, :]
    permitted = same_slot[None] & row_live[:, None, :]
    return (row_live, permitted)


def normed(values_in, gain_ln, bias_ln):
    row_mean = jnp.mean(values_in, -1, keepdims=True)
    centred = values_in - row_mean
    row_var = jnp.mean(centred * centred, -1, keepdims=True)
    return centred * lax.rsqrt(row_var + NORM_EPSILON) * gain_ln + bias_ln


def exact_gelu(values_in):
    return jax.nn.gelu(values_in, approximate=False)


def outer_sum(left, right):
    return lax.dot_general(
        left, right, (((0,), (0,)), ((), ())), preferred_element_type=jnp.float32
    )


def times_transposed(left, right):
    return lax.dot_general(
        left, right, (((1,), (1,)), ((), ())), preferred_element_type=jnp.float32
    )


def split_heads(qkv_low, permitted):
    group_count = permitted.shape[0]
    group_rows = permitted.shape[1]
    split_qkv = qkv_low.reshape(group_count, group_rows, 3, HEADS, HD)
    return (split_qkv[:, :, 0], split_qkv[:, :, 1], split_qkv[:, :, 2])


def raw_scores(queries, key_rows, permitted):
    scores = (
        jnp.einsum("gqhd,gkhd->ghqk", queries, key_rows, preferred_element_type=jnp.float32)
        * SCORE_SCALE
    )
    return jnp.where(permitted[:, None], scores, NEG_LARGE)


def attend(qkv_low, permitted):
    queries, key_rows, value_rows = split_heads(qkv_low, permitted)
    scores = raw_scores(queries, key_rows, permitted)
    row_top = jnp.max(scores, -1, keepdims=True)
    row_total = jnp.sum(jnp.exp(scores - row_top), -1, keepdims=True)
    log_total = row_top + jnp.log(row_total)
    probs = jnp.exp(scores - log_total).astype(jnp.bfloat16)
    context = jnp.einsum("ghqk,gkhd->gqhd", probs, value_rows, preferred_element_type=jnp.float32)
    return (context.reshape(qkv_low.shape[0], HEADS * HD).astype(jnp.bfloat16), log_total)


def attend_back(qkv_low, log_total, d_context, permitted):
    queries, key_rows, value_rows = split_heads(qkv_low, permitted)
    scores = raw_scores(queries, key_rows, permitted)
    probs = jnp.exp(scores - log_total)
    probs_low = probs.astype(jnp.bfloat16)
    d_heads = d_context.reshape(queries.shape)
    d_value = jnp.einsum("ghqk,gqhd->gkhd", probs_low, d_heads, preferred_element_type=jnp.float32)
    d_probs = jnp.einsum("gqhd,gkhd->ghqk", d_heads, value_rows, preferred_element_type=jnp.float32)
    d_scores = probs * (d_probs - jnp.sum(probs * d_probs, -1, keepdims=True))
    d_low = d_scores.astype(jnp.bfloat16)
    d_query = (
        jnp.einsum("ghqk,gkhd->gqhd", d_low, key_rows, preferred_element_type=jnp.float32)
        * SCORE_SCALE
    )
    d_key = (
        jnp.einsum("ghqk,gqhd->gkhd", d_low, queries, preferred_element_type=jnp.float32)
        * SCORE_SCALE
    )
    joined = jnp.stack([d_query, d_key, d_value], 2)
    return joined.reshape(qkv_low.shape[0], 3 * HEADS * HD)


def unpack(vector_row, model_width):
    pieces = [
        vector_row[segment * model_width : (segment + 1) * model_width] for segment in range(8)
    ]
    return (pieces, vector_row[8 * model_width :])


def forward_layer(hidden, weights, vector_row, permitted):
    w_qkv, w_out, w_up, w_down = weights
    model_width = hidden.shape[1]
    pieces, bias_u = unpack(vector_row, model_width)
    bias_q, bias_v, bias_o, gain_a, shift_a, bias_d, gain_b, shift_b = pieces
    h_low = hidden.astype(jnp.bfloat16)
    qkv_full = jnp.dot(h_low, w_qkv, preferred_element_type=jnp.float32) + jnp.concatenate(
        [bias_q, jnp.zeros_like(bias_q), bias_v]
    )
    qkv_low = qkv_full.astype(jnp.bfloat16)
    context, log_total = attend(qkv_low, permitted)
    mixed_a = jnp.dot(context, w_out, preferred_element_type=jnp.float32) + bias_o
    first_sum = hidden + mixed_a
    first = normed(first_sum, gain_a, shift_a)
    first_low = first.astype(jnp.bfloat16)
    inner = jnp.dot(first_low, w_up, preferred_element_type=jnp.float32) + bias_u
    active = exact_gelu(inner).astype(jnp.bfloat16)
    mixed_b = jnp.dot(active, w_down, preferred_element_type=jnp.float32) + bias_d
    second_sum = first + mixed_b
    second = normed(second_sum, gain_b, shift_b)
    saved = (h_low, qkv_low, log_total, context, first_sum, first_low, inner, active, second_sum)
    return (second, saved)


def backward_layer(d_out, saved, weights, vector_row, permitted):
    w_qkv, w_out, w_up, w_down = weights
    h_low, qkv_low, log_total, context, first_sum, first_low, inner, active, second_sum = saved
    model_width = h_low.shape[1]
    pieces, bias_u = unpack(vector_row, model_width)
    bias_q, bias_v, bias_o, gain_a, shift_a, bias_d, gain_b, shift_b = pieces
    unused_b, norm_b_back = jax.vjp(normed, second_sum, gain_b, shift_b)
    d_second_sum, d_gain_b, d_shift_b = norm_b_back(d_out)
    d_mixed_b = d_second_sum.astype(jnp.bfloat16)
    d_bias_d = jnp.sum(d_mixed_b, 0, dtype=jnp.float32)
    grad_down = outer_sum(active, d_mixed_b)
    d_active = times_transposed(d_mixed_b, w_down)
    unused_g, gelu_back = jax.vjp(exact_gelu, inner)
    d_inner = gelu_back(d_active)[0].astype(jnp.bfloat16)
    d_bias_u = jnp.sum(d_inner, 0, dtype=jnp.float32)
    grad_up = outer_sum(first_low, d_inner)
    d_first = d_second_sum + times_transposed(d_inner, w_up)
    unused_a, norm_a_back = jax.vjp(normed, first_sum, gain_a, shift_a)
    d_first_sum, d_gain_a, d_shift_a = norm_a_back(d_first)
    d_mixed_a = d_first_sum.astype(jnp.bfloat16)
    d_bias_o = jnp.sum(d_mixed_a, 0, dtype=jnp.float32)
    grad_out = outer_sum(context, d_mixed_a)
    d_context = times_transposed(d_mixed_a, w_out).astype(jnp.bfloat16)
    d_qkv = attend_back(qkv_low, log_total, d_context, permitted).astype(jnp.bfloat16)
    d_bias_qkv = jnp.sum(d_qkv, 0, dtype=jnp.float32)
    grad_qkv = outer_sum(h_low, d_qkv)
    d_hidden = d_first_sum + times_transposed(d_qkv, w_qkv)
    d_vector = jnp.concatenate(
        [
            d_bias_qkv[:model_width],
            d_bias_qkv[2 * model_width :],
            d_bias_o,
            d_gain_a,
            d_shift_a,
            d_bias_d,
            d_gain_b,
            d_shift_b,
            d_bias_u,
        ]
    )
    return (d_hidden, (grad_qkv, grad_out, grad_up, grad_down, d_vector))


def shards(tokens, valid, qkv_weight, out_weight, up_weight, down_weight, vectors, cotangent):
    group_count = valid.shape[0] // 4
    row_live, permitted = slot_layout(valid.reshape(group_count, 4))
    row_mask = row_live.reshape(-1, 1).astype(jnp.float32)
    vector_all = lax.all_gather(vectors, "fsdp", axis=1, tiled=True)
    hidden = tokens.astype(jnp.float32)
    kept_weights = []
    kept_saved = []
    for level_idx in range(LAYERS):
        weights = (
            lax.all_gather(qkv_weight[level_idx].astype(jnp.bfloat16), "fsdp", axis=0, tiled=True),
            lax.all_gather(out_weight[level_idx].astype(jnp.bfloat16), "fsdp", axis=0, tiled=True),
            lax.all_gather(up_weight[level_idx].astype(jnp.bfloat16), "fsdp", axis=0, tiled=True),
            lax.all_gather(down_weight[level_idx].astype(jnp.bfloat16), "fsdp", axis=0, tiled=True),
        )
        hidden, saved = forward_layer(hidden, weights, vector_all[level_idx], permitted)
        kept_weights.append(weights)
        kept_saved.append(saved)
    layer_out = (hidden * row_mask).astype(jnp.bfloat16)
    d_hidden = cotangent.astype(jnp.float32) * row_mask
    results = [None] * LAYERS
    for level_idx in reversed(range(LAYERS)):
        weights = (
            lax.all_gather(qkv_weight[level_idx].astype(jnp.bfloat16), "fsdp", axis=0, tiled=True),
            lax.all_gather(out_weight[level_idx].astype(jnp.bfloat16), "fsdp", axis=0, tiled=True),
            lax.all_gather(up_weight[level_idx].astype(jnp.bfloat16), "fsdp", axis=0, tiled=True),
            lax.all_gather(down_weight[level_idx].astype(jnp.bfloat16), "fsdp", axis=0, tiled=True),
        )
        d_hidden, terms = backward_layer(
            d_hidden, kept_saved[level_idx], weights, vector_all[level_idx], permitted
        )
        term_qkv, term_out, term_up, term_down, term_vector = terms
        owned = (
            lax.psum_scatter(
                term_qkv.astype(jnp.bfloat16), "fsdp", scatter_dimension=0, tiled=True
            ).astype(jnp.float32),
            lax.psum_scatter(
                term_out.astype(jnp.bfloat16), "fsdp", scatter_dimension=0, tiled=True
            ).astype(jnp.float32),
            lax.psum_scatter(
                term_up.astype(jnp.bfloat16), "fsdp", scatter_dimension=0, tiled=True
            ).astype(jnp.float32),
            lax.psum_scatter(
                term_down.astype(jnp.bfloat16), "fsdp", scatter_dimension=0, tiled=True
            ).astype(jnp.float32),
            lax.psum_scatter(
                term_vector.astype(jnp.bfloat16), "fsdp", scatter_dimension=0, tiled=True
            ).astype(jnp.float32),
        )
        shares = (
            lax.psum(owned[0].astype(jnp.bfloat16), "rep").astype(jnp.float32),
            lax.psum(owned[1].astype(jnp.bfloat16), "rep").astype(jnp.float32),
            lax.psum(owned[2].astype(jnp.bfloat16), "rep").astype(jnp.float32),
            lax.psum(owned[3].astype(jnp.bfloat16), "rep").astype(jnp.float32),
            lax.psum(owned[4].astype(jnp.bfloat16), "rep").astype(jnp.float32),
        )
        results[level_idx] = shares
    qkv_grad = jnp.stack([entry[0] for entry in results])
    out_grad = jnp.stack([entry[1] for entry in results])
    up_grad = jnp.stack([entry[2] for entry in results])
    down_grad = jnp.stack([entry[3] for entry in results])
    vector_grad = jnp.stack([entry[4] for entry in results])
    return (layer_out, d_hidden, qkv_grad, out_grad, up_grad, down_grad, vector_grad)


def solution(mesh):
    in_specs = (
        P(("rep", "fsdp"), None),
        P(("rep", "fsdp")),
        P(None, "fsdp", None),
        P(None, "fsdp", None),
        P(None, "fsdp", None),
        P(None, "fsdp", None),
        P(None, "fsdp"),
        P(("rep", "fsdp"), None),
    )
    out_specs = (
        P(("rep", "fsdp"), None),
        P(("rep", "fsdp"), None),
        P(None, "fsdp", None),
        P(None, "fsdp", None),
        P(None, "fsdp", None),
        P(None, "fsdp", None),
        P(None, "fsdp"),
    )
    return jax.shard_map(shards, mesh=mesh, in_specs=in_specs, out_specs=out_specs, check_vma=False)
```

profile of v0, /device:TPU:0, one launch (start us, length us, event | category | flops | bytes accessed | tf_op | source)
XLA Modules:
  0.0 1876.1 jit_solution(6135757692193599547)
XLA Ops:
  15.9 43.3 %all-gather.8 = f32[16,576,2]{1,2,0:T(2,128)S(1)} all-gather(f32[1,576,2]{1,2,0:T(2,128)S(1)} %bitcast.257), channel_id=1, replica_groups=mesh['rep'=2,'fsdp'=16] {'fsdp'}, dimensions={0}, use_global_device_ids=true | all-gather | bytes 78336 | tf_op jit(solution)/shard_map/all_gather | solution.py:187
  59.9 25.6 %all-gather.18.cloned.1.call-done = bf16[1,768,2304]{2,1,0:T(8,128)(2,1)} async-done(((bf16[1,48,2304]{2,1,0:T(8,128)(2,1)}), bf16[1,768,2304]{2,1,0:T(8,128)(2,1)}) %all-gather.18.cloned.1.call-update) | async-done | bytes 3538960 | tf_op jit(solution)/shard_map/all_gather | solution.py:193
  85.5 5.4 fusion.32
  91.0 3.0 copy.67
  96.1 2.6 exponential_reduce_fusion.1
  101.3 3.9 convolution_convert_fusion.11
  105.2 38.4 %all-gather.20.cloned.1.call-done = bf16[1,768,768]{2,1,0:T(8,128)(2,1)} async-done(((bf16[1,48,768]{2,1,0:T(8,128)(2,1)}), bf16[1,768,768]{2,1,0:T(8,128)(2,1)}) %all-gather.20.cloned.1.call-update) | async-done | bytes 1179664 | tf_op jit(solution)/shard_map/all_gather | solution.py:194
  146.4 80.0 %all-gather.22.cloned.1.call-done = bf16[1,768,3072]{2,1,0:T(8,128)(2,1)} async-done(((bf16[1,48,3072]{2,1,0:T(8,128)(2,1)}), bf16[1,768,3072]{2,1,0:T(8,128)(2,1)}) %all-gather.22.cloned.1.call-update) | async-done | bytes 4718608 | tf_op jit(solution)/shard_map/all_gather | solution.py:195
  226.4 20.0 %multiply_convert_fusion.3 = (bf16[512,3072]{1,0:T(8,128)(2,1)}, f32[512,3072]{1,0:T(8,128)}, f32[512,3072]{1,0:T(8,128)}) fusion(f32[3072]{0:T(1024)S(1)} %bitcast.253, bf16[1,768,3072]{2,1,0:T(8,128)(2,1)} %all-gather.22.cloned.1.call-done, f32[512,768]{1,0:T(8,128)S(1)} %get-tuple-element.107, f32[768]{0:T(1024)S(1)} %get-tuple-element.44, ...), kind=kOutput, calls=%fused_computation.33 | convolution fusion | flops 2521694208 | bytes 22042624 | tf_op jit(solution)/shard_map/dot_general | solution.py:131
  246.4 62.3 %all-gather.24.cloned.1.call-done = bf16[1,3072,768]{2,1,0:T(8,128)(2,1)} async-done(((bf16[1,192,768]{2,1,0:T(8,128)(2,1)}), bf16[1,3072,768]{2,1,0:T(8,128)(2,1)}) %all-gather.24.cloned.1.call-update) | async-done | bytes 4718608 | tf_op jit(solution)/shard_map/all_gather | solution.py:196
  308.7 6.0 fusion.115
  315.1 66.2 %all-gather.26.cloned.1.call-done = bf16[1,768,2304]{2,1,0:T(8,128)(2,1)} async-done(((bf16[1,48,2304]{2,1,0:T(8,128)(2,1)}), bf16[1,768,2304]{2,1,0:T(8,128)(2,1)}) %all-gather.26.cloned.1.call-update) | async-done | bytes 3538960 | tf_op jit(solution)/shard_map/all_gather | solution.py:193
  381.2 5.5 fusion.33
  386.7 2.8 copy.69
  396.2 3.4 convolution_convert_fusion.10
  399.6 39.0 %all-gather.28.cloned.1.call-done = bf16[1,768,768]{2,1,0:T(8,128)(2,1)} async-done(((bf16[1,48,768]{2,1,0:T(8,128)(2,1)}), bf16[1,768,768]{2,1,0:T(8,128)(2,1)}) %all-gather.28.cloned.1.call-update) | async-done | bytes 1179664 | tf_op jit(solution)/shard_map/all_gather | solution.py:194
  438.6 2.8 fusion.116
  442.9 78.4 %all-gather.30.cloned.1.call-done = bf16[1,768,3072]{2,1,0:T(8,128)(2,1)} async-done(((bf16[1,48,3072]{2,1,0:T(8,128)(2,1)}), bf16[1,768,3072]{2,1,0:T(8,128)(2,1)}) %all-gather.30.cloned.1.call-update) | async-done | bytes 4718608 | tf_op jit(solution)/shard_map/all_gather | solution.py:195
  521.4 20.8 %multiply_convert_fusion.2 = (bf16[512,3072]{1,0:T(8,128)(2,1)}, f32[512,3072]{1,0:T(8,128)}, f32[512,3072]{1,0:T(8,128)}) fusion(f32[3072]{0:T(1024)S(1)} %bitcast.255, bf16[1,768,3072]{2,1,0:T(8,128)(2,1)} %all-gather.30.cloned.1.call-done, f32[512,768]{1,0:T(8,128)} %copy-done.9, f32[768]{0:T(1024)S(1)} %get-tuple-element.36, ...), kind=kOutput, calls=%fused_computation.20 | convolution fusion | flops 2521694208 | bytes 22042624 | tf_op jit(solution)/shard_map/dot_general | solution.py:131
  542.2 61.7 %all-gather.32.cloned.1.call-done = bf16[1,3072,768]{2,1,0:T(8,128)(2,1)} async-done(((bf16[1,192,768]{2,1,0:T(8,128)(2,1)}), bf16[1,3072,768]{2,1,0:T(8,128)(2,1)}) %all-gather.32.cloned.1.call-update) | async-done | bytes 4718608 | tf_op jit(solution)/shard_map/all_gather | solution.py:196
  603.8 6.5 fusion.117
  614.7 10.3 fusion.118
  625.0 5.7 multiply_reduce_fusion.3
  637.3 7.3 convolution_bitcast_fusion.1
  644.7 9.6 multiply_reduce_fusion.1
  654.3 7.4 multiply_convert_fusion.1
  666.7 4.1 convolution_convert_fusion.4
  670.8 6.0 multiply_reduce_fusion.4
  678.3 9.6 fusion.119
  687.9 7.2 multiply_reduce_fusion.5
  701.9 11.3 multiply_reduce_fusion
  714.7 7.1 multiply_convert_fusion
  724.9 3.4 convolution_bitcast_fusion
  732.7 4.0 copy.90
  741.9 6.5 convolution_convert_fusion.2
  749.9 6.4 convolution_convert_fusion.3
  757.5 6.7 convolution_convert_fusion
  765.3 6.7 convolution_convert_fusion.1
  772.3 38.2 %reduce-scatter.27.cloned.1.call-done = bf16[48,2304]{1,0:T(8,128)(2,1)} async-done(((bf16[768,2304]{1,0:T(8,128)(2,1)}), bf16[48,2304]{1,0:T(8,128)(2,1)}) %reduce-scatter.27.cloned.1.call-update) | async-done | bytes 221200
  812.4 136.5 %reduce-scatter.25.cloned.1.call-done = bf16[48,2304]{1,0:T(8,128)(2,1)} async-done(((bf16[768,2304]{1,0:T(8,128)(2,1)}), bf16[48,2304]{1,0:T(8,128)(2,1)}) %reduce-scatter.25.cloned.1.call-update) | async-done | bytes 221200
  950.9 126.3 %reduce-scatter.15.cloned.1.call-done = bf16[48,768]{1,0:T(8,128)(2,1)} async-done(((bf16[768,768]{1,0:T(8,128)(2,1)}), bf16[48,768]{1,0:T(8,128)(2,1)}) %reduce-scatter.15.cloned.1.call-update) | async-done | bytes 73744 | tf_op jit(solution)/shard_map/reduce_scatter | solution.py:219
  1077.2 127.8 %reduce-scatter.13.cloned.1.call-done = bf16[48,768]{1,0:T(8,128)(2,1)} async-done(((bf16[768,768]{1,0:T(8,128)(2,1)}), bf16[48,768]{1,0:T(8,128)(2,1)}) %reduce-scatter.13.cloned.1.call-update) | async-done | bytes 73744 | tf_op jit(solution)/shard_map/reduce_scatter | solution.py:219
  1204.9 141.1 %reduce-scatter.19.cloned.1.call-done = bf16[48,3072]{1,0:T(8,128)(2,1)} async-done(((bf16[768,3072]{1,0:T(8,128)(2,1)}), bf16[48,3072]{1,0:T(8,128)(2,1)}) %reduce-scatter.19.cloned.1.call-update) | async-done | bytes 294928 | tf_op jit(solution)/shard_map/reduce_scatter | solution.py:222
  1346.0 142.7 %reduce-scatter.17.cloned.1.call-done = bf16[48,3072]{1,0:T(8,128)(2,1)} async-done(((bf16[768,3072]{1,0:T(8,128)(2,1)}), bf16[48,3072]{1,0:T(8,128)(2,1)}) %reduce-scatter.17.cloned.1.call-update) | async-done | bytes 294928 | tf_op jit(solution)/shard_map/reduce_scatter | solution.py:222
  1488.7 141.4 %reduce-scatter.23.cloned.1.call-done = bf16[192,768]{1,0:T(8,128)(2,1)} async-done(((bf16[3072,768]{1,0:T(8,128)(2,1)}), bf16[192,768]{1,0:T(8,128)(2,1)}) %reduce-scatter.23.cloned.1.call-update) | async-done | bytes 294928 | tf_op jit(solution)/shard_map/reduce_scatter | solution.py:225
  1630.1 142.5 %reduce-scatter.21.cloned.1.call-done = bf16[192,768]{1,0:T(8,128)(2,1)} async-done(((bf16[3072,768]{1,0:T(8,128)(2,1)}), bf16[192,768]{1,0:T(8,128)(2,1)}) %reduce-scatter.21.cloned.1.call-update) | async-done | bytes 294928 | tf_op jit(solution)/shard_map/reduce_scatter | solution.py:225
  1777.6 74.8 %all-reduce.2 = (bf16[9216]{0:T(1024)(128)(2,1)S(1)}, bf16[9216]{0:T(1024)(128)(2,1)S(1)}) all-reduce(bf16[9216]{0:T(1024)(128)(2,1)S(1)} %constant_dynamic-update-slice_fusion.1, bf16[9216]{0:T(1024)(128)(2,1)S(1)} %constant_dynamic-update-slice_fusion), channel_id=19, replica_groups=mesh['rep'=2,'fsdp'=16] {'fsdp'}, use_global_device_ids=true, to_apply=%region_57.58.clone | all-reduce | flops 18432 | bytes 73728
  1855.7 5.9 add_add_fusion.8
  (323 shorter events, 85.8 us)
Async XLA Ops:
  7.2 78.4 %all-gather.18.cloned.1.call-start = ((), (), s32[]{:S(2)}) async-start(), calls=%async_computation.14 | async-start | bytes 3760128 | tf_op jit(solution)/shard_map/all_gather | solution.py:193
  9.4 134.2 %all-gather.20.cloned.1.call-start = ((), (), s32[]{:S(2)}) async-start(), calls=%async_computation.15 | async-start | bytes 1253376 | tf_op jit(solution)/shard_map/all_gather | solution.py:194
  11.1 215.2 %all-gather.22.cloned.1.call-start = ((), (), s32[]{:S(2)}) async-start(), calls=%async_computation.16 | async-start | bytes 5013504 | tf_op jit(solution)/shard_map/all_gather | solution.py:195
  11.3 48.2 %copy-start.70 = (s32[4]{0:T(128)S(1)}, s32[4]{0:T(128)}, u32[]{:S(2)}) copy-start(s32[4]{0:T(128)} %param.9) | copy-start | bytes 52
  11.3 74.3 %copy-start.74 = (bf16[512,768]{1,0:T(8,128)(2,1)S(1)}, bf16[512,768]{1,0:T(8,128)(2,1)}, u32[]{:S(2)}) copy-start(bf16[512,768]{1,0:T(8,128)(2,1)} %param.8) | copy-start | bytes 2359300
  12.2 296.5 %all-gather.24.cloned.1.call-start = ((), (), s32[]{:S(2)}) async-start(), calls=%async_computation.17 | async-start | bytes 5013504 | tf_op jit(solution)/shard_map/all_gather | solution.py:196
  13.2 368.1 %all-gather.26.cloned.1.call-start = ((), (), s32[]{:S(2)}) async-start(), calls=%async_computation.18 | async-start | bytes 3760128 | tf_op jit(solution)/shard_map/all_gather | solution.py:193
  13.8 424.8 %all-gather.28.cloned.1.call-start = ((), (), s32[]{:S(2)}) async-start(), calls=%async_computation.19 | async-start | bytes 1253376 | tf_op jit(solution)/shard_map/all_gather | solution.py:194
  14.3 507.0 %all-gather.30.cloned.1.call-start = ((), (), s32[]{:S(2)}) async-start(), calls=%async_computation.20 | async-start | bytes 5013504 | tf_op jit(solution)/shard_map/all_gather | solution.py:195
  15.1 588.7 %all-gather.32.cloned.1.call-start = ((), (), s32[]{:S(2)}) async-start(), calls=%async_computation.21 | async-start | bytes 5013504 | tf_op jit(solution)/shard_map/all_gather | solution.py:196
  15.8 794.6 %reduce-scatter.27.cloned.1.call-start = ((), (), s32[]{:S(2)}) async-start(), calls=%async_computation.23 | async-start | bytes 3760128
  59.4 249.3 %copy-start.60 = (f32[768]{0:T(1024)}, f32[768]{0:T(1024)S(1)}, u32[]{:S(2)}) copy-start(f32[768]{0:T(1024)S(1)} %get-tuple-element.44) | copy-start | bytes 9220
  59.4 544.4 %copy-start.62 = (f32[768]{0:T(1024)}, f32[768]{0:T(1024)S(1)}, u32[]{:S(2)}) copy-start(f32[768]{0:T(1024)S(1)} %get-tuple-element.36) | copy-start | bytes 9220
  59.5 571.2 %copy-start.43 = (f32[768]{0:T(1024)}, f32[768]{0:T(1024)S(1)}, u32[]{:S(2)}) copy-start(f32[768]{0:T(1024)S(1)} %get-tuple-element.37) | copy-start | bytes 9220
  59.5 635.7 %copy-start.41 = (f32[768]{0:T(1024)}, f32[768]{0:T(1024)S(1)}, u32[]{:S(2)}) copy-start(f32[768]{0:T(1024)S(1)} %get-tuple-element.45) | copy-start | bytes 9220
  146.1 162.7 %copy-start.6 = (f32[512,768]{1,0:T(8,128)}, f32[512,768]{1,0:T(8,128)S(1)}, u32[]{:S(2)}) copy-start(f32[512,768]{1,0:T(8,128)S(1)} %get-tuple-element.107) | copy-start | bytes 4718596
  146.4 100.1 %copy-start.39 = (f32[512]{0:T(512)}, f32[512]{0:T(512)S(1)}, u32[]{:S(2)}) copy-start(f32[512]{0:T(512)S(1)} %multiply_reduce_fusion.13) | copy-start | bytes 6148
  146.4 548.8 %copy-start.47 = (f32[512]{0:T(512)}, f32[512]{0:T(512)S(1)}, u32[]{:S(2)}) copy-start(f32[512]{0:T(512)S(1)} %fusion.76) | copy-start | bytes 6148
  314.7 66.5 %copy-start.12 = (f32[512,768]{1,0:T(8,128)}, f32[512,768]{1,0:T(8,128)S(1)}, u32[]{:S(2)}) copy-start(f32[512,768]{1,0:T(8,128)S(1)} %get-tuple-element.110) | copy-start | bytes 4718596
  399.6 43.3 %copy-start.77 = (bf16[12,64,512]{2,1,0:T(8,128)(2,1)}, bf16[12,64,512]{2,1,0:T(8,128)(2,1)S(1)}, u32[]{:S(2)}) copy-start(bf16[12,64,512]{2,1,0:T(8,128)(2,1)S(1)} %convolution_convert_fusion.10) | copy-start | bytes 2359300
  441.5 189.2 %copy-start.37 = (f32[512]{0:T(512)}, f32[512]{0:T(512)S(1)}, u32[]{:S(2)}) copy-start(f32[512]{0:T(512)S(1)} %broadcast_multiply_fusion.1) | copy-start | bytes 6148
  442.9 187.8 %copy-start.49 = (f32[512]{0:T(512)}, f32[512]{0:T(512)S(1)}, u32[]{:S(2)}) copy-start(f32[512]{0:T(512)S(1)} %fusion.78) | copy-start | bytes 6148
  677.5 271.4 %reduce-scatter.25.cloned.1.call-start = ((), (), s32[]{:S(2)}) async-start(), calls=%async_computation.22 | async-start | bytes 3760128
  736.8 340.4 %reduce-scatter.15.cloned.1.call-start = ((), (), s32[]{:S(2)}) async-start(), calls=%async_computation.9 | async-start | bytes 1253376 | tf_op jit(solution)/shard_map/reduce_scatter | solution.py:219
  739.9 465.0 %reduce-scatter.13.cloned.1.call-start = ((), (), s32[]{:S(2)}) async-start(), calls=%async_computation.8 | async-start | bytes 1253376 | tf_op jit(solution)/shard_map/reduce_scatter | solution.py:219
  741.8 604.2 %reduce-scatter.19.cloned.1.call-start = ((), (), s32[]{:S(2)}) async-start(), calls=%async_computation.11 | async-start | bytes 5013504 | tf_op jit(solution)/shard_map/reduce_scatter | solution.py:222
  748.5 740.2 %reduce-scatter.17.cloned.1.call-start = ((), (), s32[]{:S(2)}) async-start(), calls=%async_computation.10 | async-start | bytes 5013504 | tf_op jit(solution)/shard_map/reduce_scatter | solution.py:222
  756.4 873.7 %reduce-scatter.23.cloned.1.call-start = ((), (), s32[]{:S(2)}) async-start(), calls=%async_computation.13 | async-start | bytes 5013504 | tf_op jit(solution)/shard_map/reduce_scatter | solution.py:225
  764.2 1008.4 %reduce-scatter.21.cloned.1.call-start = ((), (), s32[]{:S(2)}) async-start(), calls=%async_computation.12 | async-start | bytes 5013504 | tf_op jit(solution)/shard_map/reduce_scatter | solution.py:225
  772.0 1000.6 %copy-start.79 = (u32[32]{0:T(128)S(1)}, u32[32]{0:T(128)}, u32[]{:S(2)}) copy-start(u32[32]{0:T(128)} %constant.121) | copy-start | bytes 388
  772.0 1002.0 %copy-start.36 = (bf16[3,12,64]{2,1,0:T(8,128)(2,1)S(1)}, bf16[3,12,64]{2,1,0:T(8,128)(2,1)}, u32[]{:S(2)}) copy-start(bf16[3,12,64]{2,1,0:T(8,128)(2,1)} %get-tuple-element.65) | copy-start | bytes 13828
  772.0 1003.0 %copy-start.54 = (bf16[768]{0:T(1024)(128)(2,1)S(1)}, bf16[768]{0:T(1024)(128)(2,1)}, u32[]{:S(2)}) copy-start(bf16[768]{0:T(1024)(128)(2,1)} %get-tuple-element.69) | copy-start | bytes 4612
  772.0 1003.2 %copy-start.56 = (bf16[768]{0:T(1024)(128)(2,1)S(1)}, bf16[768]{0:T(1024)(128)(2,1)}, u32[]{:S(2)}) copy-start(bf16[768]{0:T(1024)(128)(2,1)} %get-tuple-element.63) | copy-start | bytes 4612
  772.0 1003.4 %copy-start.65 = (bf16[768]{0:T(1024)(128)(2,1)S(1)}, bf16[768]{0:T(1024)(128)(2,1)}, u32[]{:S(2)}) copy-start(bf16[768]{0:T(1024)(128)(2,1)} %get-tuple-element.25) | copy-start | bytes 4612
  772.1 1003.6 %copy-start.69 = (bf16[768]{0:T(1024)(128)(2,1)S(1)}, bf16[768]{0:T(1024)(128)(2,1)}, u32[]{:S(2)}) copy-start(bf16[768]{0:T(1024)(128)(2,1)} %get-tuple-element.23) | copy-start | bytes 4612
  772.1 1003.8 %copy-start.64 = (bf16[768]{0:T(1024)(128)(2,1)S(1)}, bf16[768]{0:T(1024)(128)(2,1)}, u32[]{:S(2)}) copy-start(bf16[768]{0:T(1024)(128)(2,1)} %get-tuple-element.31) | copy-start | bytes 4612
  772.1 1004.0 %copy-start.68 = (bf16[768]{0:T(1024)(128)(2,1)S(1)}, bf16[768]{0:T(1024)(128)(2,1)}, u32[]{:S(2)}) copy-start(bf16[768]{0:T(1024)(128)(2,1)} %get-tuple-element.30) | copy-start | bytes 4612
  772.1 1004.2 %copy-start.53 = (bf16[768]{0:T(1024)(128)(2,1)S(1)}, bf16[768]{0:T(1024)(128)(2,1)}, u32[]{:S(2)}) copy-start(bf16[768]{0:T(1024)(128)(2,1)} %get-tuple-element.67) | copy-start | bytes 4612
  772.1 1004.4 %copy-start.55 = (bf16[768]{0:T(1024)(128)(2,1)S(1)}, bf16[768]{0:T(1024)(128)(2,1)}, u32[]{:S(2)}) copy-start(bf16[768]{0:T(1024)(128)(2,1)} %get-tuple-element.61) | copy-start | bytes 4612
  772.1 1004.6 %copy-start.52 = (bf16[768]{0:T(1024)(128)(2,1)S(1)}, bf16[768]{0:T(1024)(128)(2,1)}, u32[]{:S(2)}) copy-start(bf16[768]{0:T(1024)(128)(2,1)} %get-tuple-element.27) | copy-start | bytes 4612
  772.1 1004.8 %copy-start.67 = (bf16[768]{0:T(1024)(128)(2,1)S(1)}, bf16[768]{0:T(1024)(128)(2,1)}, u32[]{:S(2)}) copy-start(bf16[768]{0:T(1024)(128)(2,1)} %get-tuple-element.21) | copy-start | bytes 4612
  772.1 1005.0 %copy-start.51 = (bf16[768]{0:T(1024)(128)(2,1)S(1)}, bf16[768]{0:T(1024)(128)(2,1)}, u32[]{:S(2)}) copy-start(bf16[768]{0:T(1024)(128)(2,1)} %get-tuple-element.32) | copy-start | bytes 4612
  772.1 1005.2 %copy-start.66 = (bf16[768]{0:T(1024)(128)(2,1)S(1)}, bf16[768]{0:T(1024)(128)(2,1)}, u32[]{:S(2)}) copy-start(bf16[768]{0:T(1024)(128)(2,1)} %get-tuple-element.29) | copy-start | bytes 4612
  772.1 1005.4 %copy-start.57 = (bf16[3072]{0:T(1024)(128)(2,1)S(1)}, bf16[3072]{0:T(1024)(128)(2,1)}, u32[]{:S(2)}) copy-start(bf16[3072]{0:T(1024)(128)(2,1)} %get-tuple-element.125) | copy-start | bytes 18436
  772.2 1005.4 %copy-start.58 = (bf16[3072]{0:T(1024)(128)(2,1)S(1)}, bf16[3072]{0:T(1024)(128)(2,1)}, u32[]{:S(2)}) copy-start(bf16[3072]{0:T(1024)(128)(2,1)} %get-tuple-element.127) | copy-start | bytes 18436
  772.2 1083.5 %copy-start.5 = (f32[512,768]{1,0:T(8,128)S(1)}, f32[512,768]{1,0:T(8,128)}, u32[]{:S(2)}) copy-start(f32[512,768]{1,0:T(8,128)} %copy-done.4) | copy-start | bytes 4718596
  772.2 1083.5 %copy-start.46 = (f32[512]{0:T(512)S(1)}, f32[512]{0:T(512)}, u32[]{:S(2)}) copy-start(f32[512]{0:T(512)} %copy-done.45) | copy-start | bytes 6148
  772.2 1089.4 %all-reduce.7.cloned.1.call-start = ((), (), s32[]{:S(2)}) async-start(), calls=%async_computation.24 | async-start | bytes 5013504 | tf_op jit(solution)/shard_map/psum | solution.py:233
  (58 other events, 283.3 us)
Sparse Core Ops, SparseCore 0:
  11.4 74.1 all-gather.17
  88.9 54.6 all-gather.19
  147.0 79.3 all-gather.21
  229.6 79.0 all-gather.23
  311.3 69.8 all-gather.25
  383.9 54.6 all-gather.27
  442.0 79.3 all-gather.29
  524.7 79.0 all-gather.31
  677.6 132.7 reduce-scatter.26
  815.4 133.4 reduce-scatter.24
  954.2 122.8 reduce-scatter.14
  1082.3 122.5 reduce-scatter.12
  1210.1 135.8 reduce-scatter.18
  1351.9 136.7 reduce-scatter.16
  1493.7 136.3 reduce-scatter.22
  1636.0 136.6 reduce-scatter.20
  1775.9 21.4 all-reduce.6
where the time goes:
time: 1880 us
  waiting for transfers between devices  1450 us (77%)
  matrix products  203 us (11%)
  blocking collectives  121 us (6%)
  local copies, waits for them, and re-layouts  46 us (2%)
  other arithmetic  38.7 us (2%)
    reduce_scatter x2, waiting for transfers between devices, shards(): lax.psum_scatter(term_down.astype(jnp.bfloat16), 'fsdp', scatter_dimensio...  284 us
    reduce_scatter x2, waiting for transfers between devices, shards(): lax.psum_scatter(term_up.astype(jnp.bfloat16), 'fsdp', scatter_dimension=...  284 us
    reduce_scatter x2, waiting for transfers between devices, shards(): lax.psum_scatter(term_out.astype(jnp.bfloat16), 'fsdp', scatter_dimension...  254 us
    unnamed x19, waiting for transfers between devices  177 us
    all_gather x2, waiting for transfers between devices, shards(): lax.all_gather(up_weight[level_idx].astype(jnp.bfloat16), 'fsdp', axis=0,...  158 us
    all_gather x2, waiting for transfers between devices, shards(): lax.all_gather(down_weight[level_idx].astype(jnp.bfloat16), 'fsdp', axis=...  124 us
    all_gather x2, waiting for transfers between devices, shards(): lax.all_gather(qkv_weight[level_idx].astype(jnp.bfloat16), 'fsdp', axis=0...  91.8 us
    all_gather x2, waiting for transfers between devices, shards(): lax.all_gather(out_weight[level_idx].astype(jnp.bfloat16), 'fsdp', axis=0...  77.4 us
  transfers between devices with their start and end apart: 17, of which 16 were waited for; matrix products, arithmetic and copies ran while one was open for 10% of the time, Pallas kernels for 0%

commit v1 on v0

--- a/solution.py
+++ b/solution.py
@@ -190,7 +190,15 @@
     kept_saved = []
     for level_idx in range(LAYERS):
         weights = (
-            lax.all_gather(qkv_weight[level_idx].astype(jnp.bfloat16), "fsdp", axis=0, tiled=True),
+            jnp.concatenate(
+                lax.all_to_all(
+                    jnp.stack([qkv_weight[level_idx].astype(jnp.bfloat16)] * lax.axis_size("fsdp")),
+                    "fsdp",
+                    0,
+                    0,
+                ),
+                axis=0,
+            ),
             lax.all_gather(out_weight[level_idx].astype(jnp.bfloat16), "fsdp", axis=0, tiled=True),
             lax.all_gather(up_weight[level_idx].astype(jnp.bfloat16), "fsdp", axis=0, tiled=True),
             lax.all_gather(down_weight[level_idx].astype(jnp.bfloat16), "fsdp", axis=0, tiled=True),

time: 1880 us -> 1840 us (0.979)
  waiting for transfers between devices: 1450 us -> 1320 us
  blocking collectives: 121 us -> 175 us
  starting transfers between devices: 0.94 us -> 31.9 us
    all_gather x2, waiting for transfers between devices: 91.8 us -> 6.36 us  [shards(): lax.all_gather(qkv_weight[level_idx].astype(jnp.bfloat16), 'fsdp', axis=0...]
    all_gather x1, blocking collectives: 43.3 us -> 96.3 us  [shards(): vector_all = lax.all_gather(vectors, 'fsdp', axis=1, tiled=True)]
    all_gather x2, waiting for transfers between devices: 77.4 us -> 31.9 us  [shards(): lax.all_gather(out_weight[level_idx].astype(jnp.bfloat16), 'fsdp', axis=0...]
    all_to_all x0 -> x2, starting transfers between devices: none -> 30.9 us  [shards(): lax.all_to_all(jnp.stack([qkv_weight[level_idx].astype(jnp.bfloat16)] * l...]
  transfers between devices with their start and end apart: 17 -> 19, of which waited for: 16 -> 15; matrix products, arithmetic and copies ran while one was open for 10% -> 14% of each run, Pallas kernels for 0% -> 0%
where the time goes in v1:
time: 1840 us
  waiting for transfers between devices  1320 us (72%)
  matrix products  201 us (11%)
  blocking collectives  175 us (10%)
  local copies, waits for them, and re-layouts  53 us (3%)
  other arithmetic  38.9 us (2%)
  starting transfers between devices  31.9 us (2%)
    reduce_scatter x2, waiting for transfers between devices, shards(): lax.psum_scatter(term_up.astype(jnp.bfloat16), 'fsdp', scatter_dimension=...  284 us
    reduce_scatter x2, waiting for transfers between devices, shards(): lax.psum_scatter(term_down.astype(jnp.bfloat16), 'fsdp', scatter_dimensio...  284 us
    reduce_scatter x2, waiting for transfers between devices, shards(): lax.psum_scatter(term_out.astype(jnp.bfloat16), 'fsdp', scatter_dimension...  254 us
    unnamed x19, waiting for transfers between devices  177 us
    all_gather x2, waiting for transfers between devices, shards(): lax.all_gather(up_weight[level_idx].astype(jnp.bfloat16), 'fsdp', axis=0,...  148 us
    all_gather x2, waiting for transfers between devices, shards(): lax.all_gather(down_weight[level_idx].astype(jnp.bfloat16), 'fsdp', axis=...  127 us
    all_gather x1, blocking collectives, shards(): vector_all = lax.all_gather(vectors, 'fsdp', axis=1, tiled=True)  96.3 us
    unnamed x1, blocking collectives  76 us
  transfers between devices with their start and end apart: 19, of which 15 were waited for; matrix products, arithmetic and copies ran while one was open for 14% of the time, Pallas kernels for 0%

profile of v1, /device:TPU:0, one launch (start us, length us, event | category | flops | bytes accessed | tf_op | source)
XLA Modules:
  0.0 1835.6 jit_solution(15300046695870384535)
XLA Ops:
  16.9 8.5 all-to-all-start
  26.1 96.3 %all-gather.8 = f32[16,576,2]{1,2,0:T(2,128)S(1)} all-gather(f32[1,576,2]{1,2,0:T(2,128)S(1)} %bitcast.261), channel_id=1, replica_groups=mesh['rep'=2,'fsdp'=16] {'fsdp'}, dimensions={0}, use_global_device_ids=true | all-gather | bytes 78336 | tf_op jit(solution)/shard_map/all_gather | solution.py:187
  125.7 22.4 %all-to-all-start.1 = ((bf16[16,48,2304]{2,1,0:T(8,128)(2,1)}), bf16[16,48,2304]{2,1,0:T(8,128)(2,1)}, u32[]{:S(2)}, u32[]{:S(2)}) async-start(bf16[16,48,2304]{2,1,0:T(8,128)(2,1)} %stack.139), calls=%async_computation.1 | async-start | bytes 7077888 | tf_op jit(solution)/shard_map/all_to_all | solution.py:194
  148.2 5.4 fusion.32
  153.6 3.0 copy.67
  163.9 3.9 convolution_convert_fusion.11
  170.7 69.9 %all-gather.20.cloned.1.call-done = bf16[1,768,3072]{2,1,0:T(8,128)(2,1)} async-done(((bf16[1,48,3072]{2,1,0:T(8,128)(2,1)}), bf16[1,768,3072]{2,1,0:T(8,128)(2,1)}) %all-gather.20.cloned.1.call-update) | async-done | bytes 4718608 | tf_op jit(solution)/shard_map/all_gather | solution.py:203
  240.6 20.1 %multiply_convert_fusion.3 = (bf16[512,3072]{1,0:T(8,128)(2,1)}, f32[512,3072]{1,0:T(8,128)}, f32[512,3072]{1,0:T(8,128)}) fusion(f32[3072]{0:T(1024)S(1)} %bitcast.257, bf16[1,768,3072]{2,1,0:T(8,128)(2,1)} %all-gather.20.cloned.1.call-done, f32[512,768]{1,0:T(8,128)S(1)} %get-tuple-element.107, f32[768]{0:T(1024)S(1)} %get-tuple-element.44, ...), kind=kOutput, calls=%fused_computation.33 | convolution fusion | flops 2521694208 | bytes 22042624 | tf_op jit(solution)/shard_map/dot_general | solution.py:131
  260.7 65.0 %all-gather.22.cloned.1.call-done = bf16[1,3072,768]{2,1,0:T(8,128)(2,1)} async-done(((bf16[1,192,768]{2,1,0:T(8,128)(2,1)}), bf16[1,3072,768]{2,1,0:T(8,128)(2,1)}) %all-gather.22.cloned.1.call-update) | async-done | bytes 4718608 | tf_op jit(solution)/shard_map/all_gather | solution.py:204
  325.7 6.0 fusion.113
  332.8 5.5 fusion.33
  338.4 2.8 copy.69
  347.8 3.4 convolution_convert_fusion.10
  351.2 31.9 %all-gather.24.cloned.1.call-done = bf16[1,768,768]{2,1,0:T(8,128)(2,1)} async-done(((bf16[1,48,768]{2,1,0:T(8,128)(2,1)}), bf16[1,768,768]{2,1,0:T(8,128)(2,1)}) %all-gather.24.cloned.1.call-update) | async-done | bytes 1179664 | tf_op jit(solution)/shard_map/all_gather | solution.py:202
  383.1 2.8 fusion.114
  387.4 78.2 %all-gather.26.cloned.1.call-done = bf16[1,768,3072]{2,1,0:T(8,128)(2,1)} async-done(((bf16[1,48,3072]{2,1,0:T(8,128)(2,1)}), bf16[1,768,3072]{2,1,0:T(8,128)(2,1)}) %all-gather.26.cloned.1.call-update) | async-done | bytes 4718608 | tf_op jit(solution)/shard_map/all_gather | solution.py:203
  465.7 20.8 %multiply_convert_fusion.2 = (bf16[512,3072]{1,0:T(8,128)(2,1)}, f32[512,3072]{1,0:T(8,128)}, f32[512,3072]{1,0:T(8,128)}) fusion(f32[3072]{0:T(1024)S(1)} %bitcast.259, bf16[1,768,3072]{2,1,0:T(8,128)(2,1)} %all-gather.26.cloned.1.call-done, f32[512,768]{1,0:T(8,128)} %copy-done.9, f32[768]{0:T(1024)S(1)} %get-tuple-element.36, ...), kind=kOutput, calls=%fused_computation.20 | convolution fusion | flops 2521694208 | bytes 22042624 | tf_op jit(solution)/shard_map/dot_general | solution.py:131
  486.5 61.6 %all-gather.28.cloned.1.call-done = bf16[1,3072,768]{2,1,0:T(8,128)(2,1)} async-done(((bf16[1,192,768]{2,1,0:T(8,128)(2,1)}), bf16[1,3072,768]{2,1,0:T(8,128)(2,1)}) %all-gather.28.cloned.1.call-update) | async-done | bytes 4718608 | tf_op jit(solution)/shard_map/all_gather | solution.py:204
  548.1 6.5 fusion.115
  559.0 10.4 fusion.116
  569.5 5.7 multiply_reduce_fusion.3
  581.9 11.2 multiply_reduce_fusion.1
  594.5 7.5 multiply_convert_fusion.1
  605.2 3.2 convolution_bitcast_fusion.1
  610.2 4.2 convolution_convert_fusion.4
  614.4 6.4 all-gather.30.cloned.1.call-done
  620.7 6.0 multiply_reduce_fusion.4
  628.2 9.6 fusion.117
  637.8 7.2 multiply_reduce_fusion.5
  651.8 11.3 multiply_reduce_fusion
  664.6 7.1 multiply_convert_fusion
  674.8 3.4 convolution_bitcast_fusion
  682.6 4.0 copy.90
  691.8 6.4 convolution_convert_fusion.2
  699.7 6.5 convolution_convert_fusion.3
  707.4 6.8 convolution_convert_fusion
  715.3 6.7 convolution_convert_fusion.1
  722.8 37.7 %reduce-scatter.27.cloned.1.call-done = bf16[48,2304]{1,0:T(8,128)(2,1)} async-done(((bf16[768,2304]{1,0:T(8,128)(2,1)}), bf16[48,2304]{1,0:T(8,128)(2,1)}) %reduce-scatter.27.cloned.1.call-update) | async-done | bytes 221200
  762.5 136.8 %reduce-scatter.25.cloned.1.call-done = bf16[48,2304]{1,0:T(8,128)(2,1)} async-done(((bf16[768,2304]{1,0:T(8,128)(2,1)}), bf16[48,2304]{1,0:T(8,128)(2,1)}) %reduce-scatter.25.cloned.1.call-update) | async-done | bytes 221200
  901.3 126.0 %reduce-scatter.15.cloned.1.call-done = bf16[48,768]{1,0:T(8,128)(2,1)} async-done(((bf16[768,768]{1,0:T(8,128)(2,1)}), bf16[48,768]{1,0:T(8,128)(2,1)}) %reduce-scatter.15.cloned.1.call-update) | async-done | bytes 73744 | tf_op jit(solution)/shard_map/reduce_scatter | solution.py:227
  1027.3 128.0 %reduce-scatter.13.cloned.1.call-done = bf16[48,768]{1,0:T(8,128)(2,1)} async-done(((bf16[768,768]{1,0:T(8,128)(2,1)}), bf16[48,768]{1,0:T(8,128)(2,1)}) %reduce-scatter.13.cloned.1.call-update) | async-done | bytes 73744 | tf_op jit(solution)/shard_map/reduce_scatter | solution.py:227
  1155.3 141.4 %reduce-scatter.19.cloned.1.call-done = bf16[48,3072]{1,0:T(8,128)(2,1)} async-done(((bf16[768,3072]{1,0:T(8,128)(2,1)}), bf16[48,3072]{1,0:T(8,128)(2,1)}) %reduce-scatter.19.cloned.1.call-update) | async-done | bytes 294928 | tf_op jit(solution)/shard_map/reduce_scatter | solution.py:230
  1296.7 142.7 %reduce-scatter.17.cloned.1.call-done = bf16[48,3072]{1,0:T(8,128)(2,1)} async-done(((bf16[768,3072]{1,0:T(8,128)(2,1)}), bf16[48,3072]{1,0:T(8,128)(2,1)}) %reduce-scatter.17.cloned.1.call-update) | async-done | bytes 294928 | tf_op jit(solution)/shard_map/reduce_scatter | solution.py:230
  1439.4 141.5 %reduce-scatter.23.cloned.1.call-done = bf16[192,768]{1,0:T(8,128)(2,1)} async-done(((bf16[3072,768]{1,0:T(8,128)(2,1)}), bf16[192,768]{1,0:T(8,128)(2,1)}) %reduce-scatter.23.cloned.1.call-update) | async-done | bytes 294928 | tf_op jit(solution)/shard_map/reduce_scatter | solution.py:233
  1580.9 142.3 %reduce-scatter.21.cloned.1.call-done = bf16[192,768]{1,0:T(8,128)(2,1)} async-done(((bf16[3072,768]{1,0:T(8,128)(2,1)}), bf16[192,768]{1,0:T(8,128)(2,1)}) %reduce-scatter.21.cloned.1.call-update) | async-done | bytes 294928 | tf_op jit(solution)/shard_map/reduce_scatter | solution.py:233
  1728.2 76.0 %all-reduce.2 = (bf16[9216]{0:T(1024)(128)(2,1)S(1)}, bf16[9216]{0:T(1024)(128)(2,1)S(1)}) all-reduce(bf16[9216]{0:T(1024)(128)(2,1)S(1)} %constant_dynamic-update-slice_fusion.1, bf16[9216]{0:T(1024)(128)(2,1)S(1)} %constant_dynamic-update-slice_fusion), channel_id=19, replica_groups=mesh['rep'=2,'fsdp'=16] {'fsdp'}, use_global_device_ids=true, to_apply=%region_57.58.clone | all-reduce | flops 18432 | bytes 73728
  1807.5 6.1 add_add_fusion.8
  1813.6 7.5 all-reduce.7.cloned.1.call-done
  (332 shorter events, 95.7 us)
Async XLA Ops:
  7.2 160.7 %all-gather.18.cloned.1.call-start = ((), (), s32[]{:S(2)}) async-start(), calls=%async_computation.16 | async-start | bytes 1253376 | tf_op jit(solution)/shard_map/all_gather | solution.py:202
  9.0 231.6 %all-gather.20.cloned.1.call-start = ((), (), s32[]{:S(2)}) async-start(), calls=%async_computation.17 | async-start | bytes 5013504 | tf_op jit(solution)/shard_map/all_gather | solution.py:203
  11.3 314.3 %all-gather.22.cloned.1.call-start = ((), (), s32[]{:S(2)}) async-start(), calls=%async_computation.18 | async-start | bytes 5013504 | tf_op jit(solution)/shard_map/all_gather | solution.py:204
  12.3 370.8 %all-gather.24.cloned.1.call-start = ((), (), s32[]{:S(2)}) async-start(), calls=%async_computation.19 | async-start | bytes 1253376 | tf_op jit(solution)/shard_map/all_gather | solution.py:202
  12.9 452.8 %all-gather.26.cloned.1.call-start = ((), (), s32[]{:S(2)}) async-start(), calls=%async_computation.20 | async-start | bytes 5013504 | tf_op jit(solution)/shard_map/all_gather | solution.py:203
  13.5 534.5 %all-gather.28.cloned.1.call-start = ((), (), s32[]{:S(2)}) async-start(), calls=%async_computation.21 | async-start | bytes 5013504 | tf_op jit(solution)/shard_map/all_gather | solution.py:204
  16.9 106.4 %copy-start.72 = (s32[4]{0:T(128)S(1)}, s32[4]{0:T(128)}, u32[]{:S(2)}) copy-start(s32[4]{0:T(128)} %param.9) | copy-start | bytes 52
  16.9 106.8 %copy-start.20 = (bf16[1,48,2304]{2,1,0:T(8,128)(2,1)S(1)}, bf16[1,48,2304]{2,1,0:T(8,128)(2,1)}, u32[]{:S(2)}) copy-start(bf16[1,48,2304]{2,1,0:T(8,128)(2,1)} %get-tuple-element.89) | copy-start | bytes 663556
  16.9 106.8 %all-to-all-start = ((bf16[16,48,2304]{2,1,0:T(8,128)(2,1)}), bf16[16,48,2304]{2,1,0:T(8,128)(2,1)}, u32[]{:S(2)}, u32[]{:S(2)}) async-start(bf16[16,48,2304]{2,1,0:T(8,128)(2,1)} %stack.137), calls=%async_computation | async-start | bytes 7077888 | tf_op jit(solution)/shard_map/all_to_all | solution.py:194
  25.4 595.4 %all-gather.30.cloned.1.call-start = ((), (), s32[]{:S(2)}) async-start(), calls=%async_computation.22 | async-start | bytes 3760128 | tf_op jit(solution)/shard_map/all_gather | solution.py:214
  123.2 202.4 %copy-start.62 = (f32[768]{0:T(1024)}, f32[768]{0:T(1024)S(1)}, u32[]{:S(2)}) copy-start(f32[768]{0:T(1024)S(1)} %get-tuple-element.44) | copy-start | bytes 9220
  123.2 424.8 %copy-start.64 = (f32[768]{0:T(1024)}, f32[768]{0:T(1024)S(1)}, u32[]{:S(2)}) copy-start(f32[768]{0:T(1024)S(1)} %get-tuple-element.36) | copy-start | bytes 9220
  123.2 452.0 %copy-start.44 = (f32[768]{0:T(1024)}, f32[768]{0:T(1024)S(1)}, u32[]{:S(2)}) copy-start(f32[768]{0:T(1024)S(1)} %get-tuple-element.37) | copy-start | bytes 9220
  123.2 521.8 %copy-start.42 = (f32[768]{0:T(1024)}, f32[768]{0:T(1024)S(1)}, u32[]{:S(2)}) copy-start(f32[768]{0:T(1024)S(1)} %get-tuple-element.45) | copy-start | bytes 9220
  125.7 206.3 %all-to-all-start.1 = ((bf16[16,48,2304]{2,1,0:T(8,128)(2,1)}), bf16[16,48,2304]{2,1,0:T(8,128)(2,1)}, u32[]{:S(2)}, u32[]{:S(2)}) async-start(bf16[16,48,2304]{2,1,0:T(8,128)(2,1)} %stack.139), calls=%async_computation.1 | async-start | bytes 7077888 | tf_op jit(solution)/shard_map/all_to_all | solution.py:194
  148.1 612.4 %reduce-scatter.27.cloned.1.call-start = ((), (), s32[]{:S(2)}) async-start(), calls=%async_computation.25 | async-start | bytes 3760128
  170.3 155.3 %copy-start.6 = (f32[512,768]{1,0:T(8,128)}, f32[512,768]{1,0:T(8,128)S(1)}, u32[]{:S(2)}) copy-start(f32[512,768]{1,0:T(8,128)S(1)} %get-tuple-element.107) | copy-start | bytes 4718596
  170.6 90.0 %copy-start.40 = (f32[512]{0:T(512)}, f32[512]{0:T(512)S(1)}, u32[]{:S(2)}) copy-start(f32[512]{0:T(512)S(1)} %multiply_reduce_fusion.13) | copy-start | bytes 6148
  170.7 474.4 %copy-start.49 = (f32[512]{0:T(512)}, f32[512]{0:T(512)S(1)}, u32[]{:S(2)}) copy-start(f32[512]{0:T(512)S(1)} %fusion.74) | copy-start | bytes 6148
  385.9 189.3 %copy-start.38 = (f32[512]{0:T(512)}, f32[512]{0:T(512)S(1)}, u32[]{:S(2)}) copy-start(f32[512]{0:T(512)S(1)} %broadcast_multiply_fusion.1) | copy-start | bytes 6148
  387.4 187.8 %copy-start.51 = (f32[512]{0:T(512)}, f32[512]{0:T(512)S(1)}, u32[]{:S(2)}) copy-start(f32[512]{0:T(512)S(1)} %fusion.76) | copy-start | bytes 6148
  627.4 271.9 %reduce-scatter.25.cloned.1.call-start = ((), (), s32[]{:S(2)}) async-start(), calls=%async_computation.24 | async-start | bytes 3760128
  686.7 340.6 %reduce-scatter.15.cloned.1.call-start = ((), (), s32[]{:S(2)}) async-start(), calls=%async_computation.11 | async-start | bytes 1253376 | tf_op jit(solution)/shard_map/reduce_scatter | solution.py:227
  689.8 465.4 %reduce-scatter.13.cloned.1.call-start = ((), (), s32[]{:S(2)}) async-start(), calls=%async_computation.10 | async-start | bytes 1253376 | tf_op jit(solution)/shard_map/reduce_scatter | solution.py:227
  691.7 605.0 %reduce-scatter.19.cloned.1.call-start = ((), (), s32[]{:S(2)}) async-start(), calls=%async_computation.13 | async-start | bytes 5013504 | tf_op jit(solution)/shard_map/reduce_scatter | solution.py:230
  698.3 741.1 %reduce-scatter.17.cloned.1.call-start = ((), (), s32[]{:S(2)}) async-start(), calls=%async_computation.12 | async-start | bytes 5013504 | tf_op jit(solution)/shard_map/reduce_scatter | solution.py:230
  706.3 874.6 %reduce-scatter.23.cloned.1.call-start = ((), (), s32[]{:S(2)}) async-start(), calls=%async_computation.15 | async-start | bytes 5013504 | tf_op jit(solution)/shard_map/reduce_scatter | solution.py:233
  714.2 1009.0 %reduce-scatter.21.cloned.1.call-start = ((), (), s32[]{:S(2)}) async-start(), calls=%async_computation.14 | async-start | bytes 5013504 | tf_op jit(solution)/shard_map/reduce_scatter | solution.py:233
  722.0 1001.2 %copy-start.81 = (u32[32]{0:T(128)S(1)}, u32[32]{0:T(128)}, u32[]{:S(2)}) copy-start(u32[32]{0:T(128)} %constant.121) | copy-start | bytes 388
  722.0 1002.7 %copy-start.37 = (bf16[3,12,64]{2,1,0:T(8,128)(2,1)S(1)}, bf16[3,12,64]{2,1,0:T(8,128)(2,1)}, u32[]{:S(2)}) copy-start(bf16[3,12,64]{2,1,0:T(8,128)(2,1)} %get-tuple-element.65) | copy-start | bytes 13828
  722.0 1003.6 %copy-start.56 = (bf16[768]{0:T(1024)(128)(2,1)S(1)}, bf16[768]{0:T(1024)(128)(2,1)}, u32[]{:S(2)}) copy-start(bf16[768]{0:T(1024)(128)(2,1)} %get-tuple-element.69) | copy-start | bytes 4612
  722.0 1003.8 %copy-start.58 = (bf16[768]{0:T(1024)(128)(2,1)S(1)}, bf16[768]{0:T(1024)(128)(2,1)}, u32[]{:S(2)}) copy-start(bf16[768]{0:T(1024)(128)(2,1)} %get-tuple-element.63) | copy-start | bytes 4612
  722.0 1004.0 %copy-start.67 = (bf16[768]{0:T(1024)(128)(2,1)S(1)}, bf16[768]{0:T(1024)(128)(2,1)}, u32[]{:S(2)}) copy-start(bf16[768]{0:T(1024)(128)(2,1)} %get-tuple-element.25) | copy-start | bytes 4612
  722.0 1004.2 %copy-start.71 = (bf16[768]{0:T(1024)(128)(2,1)S(1)}, bf16[768]{0:T(1024)(128)(2,1)}, u32[]{:S(2)}) copy-start(bf16[768]{0:T(1024)(128)(2,1)} %get-tuple-element.23) | copy-start | bytes 4612
  722.1 1004.4 %copy-start.66 = (bf16[768]{0:T(1024)(128)(2,1)S(1)}, bf16[768]{0:T(1024)(128)(2,1)}, u32[]{:S(2)}) copy-start(bf16[768]{0:T(1024)(128)(2,1)} %get-tuple-element.31) | copy-start | bytes 4612
  722.1 1004.6 %copy-start.70 = (bf16[768]{0:T(1024)(128)(2,1)S(1)}, bf16[768]{0:T(1024)(128)(2,1)}, u32[]{:S(2)}) copy-start(bf16[768]{0:T(1024)(128)(2,1)} %get-tuple-element.30) | copy-start | bytes 4612
  722.1 1004.9 %copy-start.55 = (bf16[768]{0:T(1024)(128)(2,1)S(1)}, bf16[768]{0:T(1024)(128)(2,1)}, u32[]{:S(2)}) copy-start(bf16[768]{0:T(1024)(128)(2,1)} %get-tuple-element.67) | copy-start | bytes 4612
  722.1 1005.1 %copy-start.57 = (bf16[768]{0:T(1024)(128)(2,1)S(1)}, bf16[768]{0:T(1024)(128)(2,1)}, u32[]{:S(2)}) copy-start(bf16[768]{0:T(1024)(128)(2,1)} %get-tuple-element.61) | copy-start | bytes 4612
  722.1 1005.3 %copy-start.54 = (bf16[768]{0:T(1024)(128)(2,1)S(1)}, bf16[768]{0:T(1024)(128)(2,1)}, u32[]{:S(2)}) copy-start(bf16[768]{0:T(1024)(128)(2,1)} %get-tuple-element.27) | copy-start | bytes 4612
  722.1 1005.5 %copy-start.69 = (bf16[768]{0:T(1024)(128)(2,1)S(1)}, bf16[768]{0:T(1024)(128)(2,1)}, u32[]{:S(2)}) copy-start(bf16[768]{0:T(1024)(128)(2,1)} %get-tuple-element.21) | copy-start | bytes 4612
  722.1 1005.7 %copy-start.53 = (bf16[768]{0:T(1024)(128)(2,1)S(1)}, bf16[768]{0:T(1024)(128)(2,1)}, u32[]{:S(2)}) copy-start(bf16[768]{0:T(1024)(128)(2,1)} %get-tuple-element.32) | copy-start | bytes 4612
  722.1 1005.9 %copy-start.68 = (bf16[768]{0:T(1024)(128)(2,1)S(1)}, bf16[768]{0:T(1024)(128)(2,1)}, u32[]{:S(2)}) copy-start(bf16[768]{0:T(1024)(128)(2,1)} %get-tuple-element.29) | copy-start | bytes 4612
  722.1 1006.1 %copy-start.59 = (bf16[3072]{0:T(1024)(128)(2,1)S(1)}, bf16[3072]{0:T(1024)(128)(2,1)}, u32[]{:S(2)}) copy-start(bf16[3072]{0:T(1024)(128)(2,1)} %get-tuple-element.125) | copy-start | bytes 18436
  722.1 1006.1 %copy-start.60 = (bf16[3072]{0:T(1024)(128)(2,1)S(1)}, bf16[3072]{0:T(1024)(128)(2,1)}, u32[]{:S(2)}) copy-start(bf16[3072]{0:T(1024)(128)(2,1)} %get-tuple-element.127) | copy-start | bytes 18436
  722.2 1085.3 %copy-start.5 = (f32[512,768]{1,0:T(8,128)S(1)}, f32[512,768]{1,0:T(8,128)}, u32[]{:S(2)}) copy-start(f32[512,768]{1,0:T(8,128)} %copy-done.4) | copy-start | bytes 4718596
  722.2 1085.3 %copy-start.48 = (f32[512]{0:T(512)S(1)}, f32[512]{0:T(512)}, u32[]{:S(2)}) copy-start(f32[512]{0:T(512)} %copy-done.47) | copy-start | bytes 6148
  722.2 1085.3 %all-gather.32.cloned.1.call-start = ((), (), s32[]{:S(2)}) async-start(), calls=%async_computation.23 | async-start | bytes 3760128 | tf_op jit(solution)/shard_map/all_gather | solution.py:214
  722.8 1098.4 %all-reduce.7.cloned.1.call-start = ((), (), s32[]{:S(2)}) async-start(), calls=%async_computation.26 | async-start | bytes 5013504 | tf_op jit(solution)/shard_map/psum | solution.py:241
  (62 other events, 349.3 us)
Sparse Core Ops, SparseCore 0:
  11.4 99.3 all-gather.17
  114.1 126.4 all-gather.19
  244.0 81.6 all-gather.21
  328.3 54.7 all-gather.23
  386.3 79.3 all-gather.25
  468.9 79.0 all-gather.27
  550.8 69.8 all-gather.29
  627.5 132.9 reduce-scatter.26
  765.6 133.6 reduce-scatter.24
  904.4 122.7 reduce-scatter.14
  1032.6 122.5 reduce-scatter.12
  1160.3 136.3 reduce-scatter.18
  1302.7 136.6 reduce-scatter.16
  1444.4 136.4 reduce-scatter.22
  1586.7 136.4 reduce-scatter.20
  1725.9 70.8 all-gather.31
  1800.1 21.0 all-reduce.6
